TPU v7x, 256 devices: a whole 4x4x8 slice. The times are simulated.
256 devices in a mesh: samp: 8 (over y, core), par: 32 (over z, x).
Axes of the slice: x: 4, y: 4, z: 8, core: 2. Of those that a mesh axis runs over, the one named last changes fastest.
Arguments:
- jacobian: bfloat16 [8192, 65536], P(('samp', 'par')), as said below
- sample_slot: int32 [8192], P(('samp', 'par')), may hold values from 0 to 1023, as said below
- panel_index: int32 [1], replicated, may hold values from 0 to 8191
- shift_value: float32 [1], replicated, may hold values from 0.1 to 1
Outputs:
- cholesky_panel: float32 [8192, 1024], P(('samp', 'par'))
Inputs may be any that keep to these rules, and one draw needn't show every extreme that they name: Within each group (samples g * 1024 to (g + 1) * 1024 - 1), sample_slot is a permutation of 0 to 1023. `jacobian`: finite values.
All inputs are finite; a program needn't handle non-finite values.
Results may differ from a plain program's by a relative error of at most 0.0003.
Values may be sent and summed in bfloat16 or wider, within the bound.
A program may use at most 128 MiB of HBM per device.

v0:
```python
import jax
import jax.numpy as jnp
from jax import lax
from jax.sharding import Mesh
from jax.sharding import PartitionSpec as P

PAR = ("par_0", "par_1")
SAMP_PAR = ("samp", "par_0", "par_1")


def sent_to_all(shard, axis):
    peers = lax.axis_size(axis)
    return lax.all_to_all(
        jnp.broadcast_to(shard[None], (peers, *shard.shape)), axis, 0, 0, tiled=True
    )


def laid_out(tiles, dim):
    tiles = jnp.moveaxis(tiles, 0, dim)
    dims = tiles.shape
    return tiles.reshape(*dims[:dim], dims[dim] * dims[dim + 1], *dims[dim + 2 :])


def gather_directly(shard, axis, dim):
    tiles = sent_to_all(shard, axis)
    return laid_out(tiles, dim)


def padded_to(lines, peers):
    spare = -len(lines) % peers
    return jnp.pad(lines, [(0, spare)] + [(0, 0)] * (lines.ndim - 1))


def spread(shard, axis, root):
    lines = jnp.where(lax.axis_index(axis) == root, shard, jnp.zeros_like(shard)).reshape(
        -1, *shard.shape[1:][-1:]
    )
    padded = padded_to(lines, lax.axis_size(axis))
    own = lax.psum_scatter(padded, axis, scatter_dimension=0, tiled=True)
    return lax.all_gather(own, axis, axis=0, tiled=True)[: len(lines)].reshape(shard.shape)


def sum_by_axis(shard, axes, dim):
    if not axes:
        return shard
    nearer = lax.psum_scatter(shard, axes[0], scatter_dimension=dim, tiled=True)
    return sum_by_axis(nearer, axes[1:], dim)


def invert_factor(block, identity_matrix):
    factor = jnp.linalg.cholesky(block)
    return lax.linalg.triangular_solve(factor, identity_matrix, left_side=True, lower=True)


def on_device(jacobian, sample_slot, panel_index, shift_value):
    arrived = lax.all_to_all(jacobian, PAR, split_axis=1, concat_axis=0, tiled=True)
    own_slots = gather_directly(sample_slot, PAR, 0)
    inverse = jnp.argsort(own_slots)
    ordered = jnp.take(arrived, inverse, axis=0)
    group_width = ordered.shape[0]
    pivot_group = panel_index[0] // group_width
    rotation = panel_index[0] % group_width
    pivot_rows = jnp.roll(spread(ordered, "samp", pivot_group), -rotation, axis=0)
    partial_gram = lax.dot_general(
        ordered, pivot_rows, (((1,), (1,)), ((), ())), preferred_element_type=jnp.float32
    )
    share = group_width // lax.axis_size(PAR)
    samples = group_width * lax.axis_size("samp")
    identity_matrix = jnp.eye(group_width, dtype=jnp.float32)
    shifted_eye = jnp.roll(identity_matrix, -rotation, axis=1)
    on_pivot = (lax.axis_index("samp") == pivot_group).astype(jnp.float32)
    shift_term = shift_value[0] * on_pivot
    start = lax.axis_index(PAR) * share
    summed = sum_by_axis(partial_gram, PAR, 0)
    band = lax.dynamic_slice_in_dim(shifted_eye, start, share, 0)
    my_rows = summed / samples + shift_term * band
    pivot_partial = lax.dot_general(
        pivot_rows, pivot_rows, (((1,), (1,)), ((), ())), preferred_element_type=jnp.float32
    )
    pivot_sum = lax.psum(pivot_partial, PAR)
    pivot_block = pivot_sum / samples + shift_value[0] * identity_matrix
    inverse_factor = invert_factor(pivot_block, identity_matrix)
    return lax.dot_general(
        my_rows,
        inverse_factor,
        (((1,), (1,)), ((), ())),
        precision=lax.Precision.HIGHEST,
        preferred_element_type=jnp.float32,
    )


def solution(mesh):
    torus = Mesh(mesh.devices.reshape(mesh.shape["samp"], 8, 4), ("samp", "par_0", "par_1"))
    return jax.shard_map(
        on_device,
        mesh=torus,
        in_specs=(P(SAMP_PAR, None), P(SAMP_PAR), P(), P()),
        out_specs=P(SAMP_PAR, None),
        check_vma=False,
    )
```

profile of v0, /device:TPU:2, one launch (start us, length us, event | category | flops | bytes accessed | tf_op | source)
XLA Modules:
  0.0 794.7 jit_solution(5502740099929445992)
XLA Ops:
  7.8 11.6 %all-to-all-start = ((s32[32,1,32]{2,1,0:T(1,128)}), s32[32,1,32]{2,1,0:T(1,128)S(1)}, u32[]{:S(2)}, u32[]{:S(2)}) async-start(s32[32,1,32]{2,1,0:T(1,128)} %broadcast_in_dim.23), calls=%async_computation | async-start | bytes 32768 | tf_op jit(solution)/shard_map/all_to_all | solution.py:13
  27.9 6.1 all-to-all-start.1
  40.4 86.5 %all-to-all-done.1 = bf16[32,32,2048]{2,0,1:T(8,128)(2,1)} async-done(((bf16[32,32,2048]{2,0,1:T(8,128)(2,1)}), bf16[32,32,2048]{2,0,1:T(8,128)(2,1)}, u32[]{:S(2)}, u32[]{:S(2)}) %all-to-all-start.1) | async-done | bytes 4194336 | tf_op jit(solution)/shard_map/all_to_all | solution.py:56
  127.0 11.6 %gather_fusion = bf16[1024,2048]{1,0:T(8,128)(2,1)} fusion(bf16[1024,2048]{1,0:T(8,128)(2,1)} %bitcast.1, s32[1024]{0:T(1024)S(1)} %fusion.77), kind=kCustom, calls=%fused_computation | custom fusion | bytes 8392704 | tf_op jit(solution)/shard_map/jit(_take)/gather | solution.py:59
  142.5 39.4 %reduce-scatter.6.cloned.1.call-done = bf16[128,2048]{1,0:T(8,128)(2,1)} async-done(((bf16[1024,2048]{1,0:T(8,128)(2,1)}), bf16[128,2048]{1,0:T(8,128)(2,1)}) %reduce-scatter.6.cloned.1.call-update) | async-done | bytes 524304 | tf_op jit(solution)/shard_map/reduce_scatter | solution.py:39
  182.0 35.3 %all-gather.2.cloned.1.call-done = bf16[1024,2048]{1,0:T(8,128)(2,1)} async-done(((bf16[128,2048]{1,0:T(8,128)(2,1)}), bf16[1024,2048]{1,0:T(8,128)(2,1)}) %all-gather.2.cloned.1.call-update) | async-done | bytes 4194320 | tf_op jit(solution)/shard_map/all_gather | solution.py:40
  217.3 13.5 %fusion.85 = f32[1024,1024]{0,1:T(8,128)} fusion(s32[]{:T(128)S(6)} %select_n.64, bf16[1024,2048]{1,0:T(8,128)(2,1)} %all-gather.2.cloned.1.call-done), kind=kOutput, calls=%fused_computation.182 | convolution fusion | flops 4303355904 | bytes 8388612 | tf_op jit(solution)/shard_map/dot_general | solution.py:77
  235.5 9.8 %fusion.11 = f32[1024,1024]{0,1:T(8,128)} fusion(bf16[1024,2048]{1,0:T(8,128)(2,1)S(1)} %copy-done.2, pred[1024]{0:T(1024)(128)(4,1)S(1)} %compare_and_fusion, s32[]{:T(128)S(6)} %select_n.64, bf16[1024,2048]{1,0:T(8,128)(2,1)} %all-gather.2.cloned.1.call-done), kind=kOutput, calls=%fused_computation.26 | convolution fusion | flops 4305453056 | bytes 12583940 | tf_op jit(solution)/shard_map/dot_general | solution.py:64
  245.3 148.3 %all-reduce.3.cloned.1.call-done = f32[1024,1024]{0,1:T(8,128)} async-done(((f32[1024,1024]{0,1:T(8,128)}), f32[1024,1024]{0,1:T(8,128)}) %all-reduce.3.cloned.1.call-update) | async-done | bytes 4194320 | tf_op jit(solution)/shard_map/psum | solution.py:80
  393.6 5.0 select_add_fusion
  398.5 5.4 copy.26
  410.7 11.7 %cholesky.222 = f32[128,128]{1,0:T(8,128)S(1)} custom-call(f32[128,128]{1,0:T(8,128)S(1)} %cholesky.577), custom_call_target="Cholesky" | custom-call | tf_op jit(solution)/shard_map/jit(cholesky)/cholesky | solution.py:51
  422.6 9.8 %custom-call.62 = f32[1,128,128]{1,2,0:T(8,128)S(1)} custom-call(f32[1,128,128]{2,1,0:T(8,128)S(1)} %get-tuple-element.71), custom_call_target="InvertDiagBlocksLowerTriangular" | custom-call | tf_op jit(solution)/shard_map/jit(cholesky)/cholesky | solution.py:51
  435.7 11.7 %cholesky.243 = f32[128,128]{1,0:T(8,128)S(1)} custom-call(f32[128,128]{1,0:T(8,128)S(1)} %cholesky.581), custom_call_target="Cholesky" | custom-call | tf_op jit(solution)/shard_map/jit(cholesky)/cholesky | solution.py:51
  448.0 9.8 %custom-call.63 = f32[1,128,128]{1,2,0:T(8,128)S(1)} custom-call(f32[1,128,128]{2,1,0:T(8,128)S(1)} %get-tuple-element.69), custom_call_target="InvertDiagBlocksLowerTriangular" | custom-call | tf_op jit(solution)/shard_map/jit(cholesky)/cholesky | solution.py:51
  463.3 11.7 %cholesky.466 = f32[128,128]{1,0:T(8,128)S(1)} custom-call(f32[128,128]{1,0:T(8,128)S(1)} %cholesky.586), custom_call_target="Cholesky" | custom-call | tf_op jit(solution)/shard_map/jit(cholesky)/cholesky | solution.py:51
  475.8 9.8 %custom-call.64 = f32[1,128,128]{1,2,0:T(8,128)S(1)} custom-call(f32[1,128,128]{2,1,0:T(8,128)S(1)} %get-tuple-element.67), custom_call_target="InvertDiagBlocksLowerTriangular" | custom-call | tf_op jit(solution)/shard_map/jit(cholesky)/cholesky | solution.py:51
  490.1 11.7 %cholesky.485 = f32[128,128]{1,0:T(8,128)S(1)} custom-call(f32[128,128]{1,0:T(8,128)S(1)} %cholesky.591), custom_call_target="Cholesky" | custom-call | tf_op jit(solution)/shard_map/jit(cholesky)/cholesky | solution.py:51
  502.6 9.8 %custom-call.65 = f32[1,128,128]{1,2,0:T(8,128)S(1)} custom-call(f32[1,128,128]{2,1,0:T(8,128)S(1)} %get-tuple-element.65), custom_call_target="InvertDiagBlocksLowerTriangular" | custom-call | tf_op jit(solution)/shard_map/jit(cholesky)/cholesky | solution.py:51
  516.7 12.1 %cholesky.504 = f32[128,128]{1,0:T(8,128)S(1)} custom-call(f32[128,128]{1,0:T(8,128)S(1)} %cholesky.596), custom_call_target="Cholesky" | custom-call | tf_op jit(solution)/shard_map/jit(cholesky)/cholesky | solution.py:51
  529.6 9.8 %custom-call.66 = f32[1,128,128]{1,2,0:T(8,128)S(1)} custom-call(f32[1,128,128]{2,1,0:T(8,128)S(1)} %get-tuple-element.63), custom_call_target="InvertDiagBlocksLowerTriangular" | custom-call | tf_op jit(solution)/shard_map/jit(cholesky)/cholesky | solution.py:51
  543.7 11.7 %cholesky.524 = f32[128,128]{1,0:T(8,128)S(1)} custom-call(f32[128,128]{1,0:T(8,128)S(1)} %cholesky.601), custom_call_target="Cholesky" | custom-call | tf_op jit(solution)/shard_map/jit(cholesky)/cholesky | solution.py:51
  556.1 9.8 %custom-call.67 = f32[1,128,128]{1,2,0:T(8,128)S(1)} custom-call(f32[1,128,128]{2,1,0:T(8,128)S(1)} %get-tuple-element.61), custom_call_target="InvertDiagBlocksLowerTriangular" | custom-call | tf_op jit(solution)/shard_map/jit(cholesky)/cholesky | solution.py:51
  569.8 11.7 %cholesky.544 = f32[128,128]{1,0:T(8,128)S(1)} custom-call(f32[128,128]{1,0:T(8,128)S(1)} %cholesky.606), custom_call_target="Cholesky" | custom-call | tf_op jit(solution)/shard_map/jit(cholesky)/cholesky | solution.py:51
  582.3 9.8 %custom-call.68 = f32[1,128,128]{1,2,0:T(8,128)S(1)} custom-call(f32[1,128,128]{2,1,0:T(8,128)S(1)} %get-tuple-element.59), custom_call_target="InvertDiagBlocksLowerTriangular" | custom-call | tf_op jit(solution)/shard_map/jit(cholesky)/cholesky | solution.py:51
  595.1 11.7 %cholesky.562 = f32[128,128]{1,0:T(8,128)S(1)} custom-call(f32[128,128]{1,0:T(8,128)S(1)} %convolution_subtract_fusion.11), custom_call_target="Cholesky" | custom-call | tf_op jit(solution)/shard_map/jit(cholesky)/cholesky | solution.py:51
  622.1 24.0 %while.1 = (s32[]{:T(128)}, f32[1024,1024]{0,1:T(8,128)}, s32[8,2]{0,1:T(2,128)S(1)}, f32[8,128,128]{2,1,0:T(8,128)S(1)}, s32[]{:T(128)}) while((s32[]{:T(128)}, f32[1024,1024]{0,1:T(8,128)}, s32[8,2]{0,1:T(2,128)S(1)}, f32[8,128,128]{2,1,0:T(8,128)S(1)}, s32[]{:T(128)}) %tuple.51), condition=%wide.while_cond, body=%wide.while_body.sunk | while | flops 2 | bytes 393329 | solution.py:52
  646.0 79.6 %custom-call.69 = f32[8,128,128]{1,2,0:T(8,128)} custom-call(f32[8,128,128]{2,1,0:T(8,128)S(1)} %get-tuple-element.14), custom_call_target="InvertDiagBlocksLowerTriangular" | custom-call | tf_op jit(solution)/shard_map/triangular_solve | solution.py:52
  749.4 5.4 convolution_subtract_fusion.2
  758.6 6.2 convolution_subtract_fusion.1
  767.3 8.6 %convolution_subtract_fusion.3 = f32[128,1024]{0,1:T(8,128)S(1)} fusion(f32[896,1024]{1,0:T(8,128)} %get-tuple-element.33, f32[1024,1024]{0,1:T(8,128)} %fusion.2, f32[1024,1024]{0,1:T(8,128)} %get-tuple-element.132), kind=kOutput, calls=%fused_computation.40 | convolution fusion | flops 1409417216 | bytes 5177344 | tf_op jit(solution)/shard_map/triangular_solve | solution.py:52
  780.3 7.6 fusion.33
  (148 shorter events, 131.6 us)
Async XLA Ops:
  7.8 20.1 %all-to-all-start = ((s32[32,1,32]{2,1,0:T(1,128)}), s32[32,1,32]{2,1,0:T(1,128)S(1)}, u32[]{:S(2)}, u32[]{:S(2)}) async-start(s32[32,1,32]{2,1,0:T(1,128)} %broadcast_in_dim.23), calls=%async_computation | async-start | bytes 32768 | tf_op jit(solution)/shard_map/all_to_all | solution.py:13
  27.9 99.1 %all-to-all-start.1 = ((bf16[32,32,2048]{2,0,1:T(8,128)(2,1)}), bf16[32,32,2048]{2,0,1:T(8,128)(2,1)}, u32[]{:S(2)}, u32[]{:S(2)}) async-start(bf16[32,32,2048]{2,0,1:T(8,128)(2,1)} %bitcast.117), calls=%async_computation.1 | async-start | bytes 8388608 | tf_op jit(solution)/shard_map/all_to_all | solution.py:56
  34.0 147.9 %reduce-scatter.6.cloned.1.call-start = ((), (), s32[]{:S(2)}) async-start(), calls=%async_computation.5 | async-start | bytes 4718592 | tf_op jit(solution)/shard_map/reduce_scatter | solution.py:39
  142.5 74.8 %all-gather.2.cloned.1.call-start = ((), (), s32[]{:S(2)}) async-start(), calls=%async_computation.6 | async-start | bytes 4718592 | tf_op jit(solution)/shard_map/all_gather | solution.py:40
  182.0 211.6 %all-reduce.3.cloned.1.call-start = ((), (), s32[]{:S(2)}) async-start(), calls=%async_computation.8 | async-start | bytes 8388608 | tf_op jit(solution)/shard_map/psum | solution.py:80
  230.8 525.7 %reduce-scatter.8.cloned.1.call-start = ((), (), s32[]{:S(2)}) async-start(), calls=%async_computation.7 | async-start | bytes 4718592 | tf_op jit(solution)/shard_map/reduce_scatter | solution.py:46
  231.7 3.7 copy-start.2
  245.2 534.0 %reduce-scatter.10.cloned.1.call-start = ((), (), s32[]{:S(2)}) async-start(), calls=%async_computation.9 | async-start | bytes 655360
  408.8 2.0 copy-start.3
  458.9 2.0 copy-start
  725.6 7.4 copy-start.1
  728.2 7.6 copy-start.4
Sparse Core Ops, SparseCore 0:
  142.6 39.2 reduce-scatter.5
  183.8 33.4 all-gather.1
  230.9 162.5 all-reduce.2
  396.0 54.0 reduce-scatter.7
  758.7 20.4 reduce-scatter.9
where the time goes:
time: 806 us; the launch traced here: 795 us
  waiting for transfers between devices  314 us (39%)
  other arithmetic  274 us (34%)
  matrix products  107 us (13%)
  local copies, waits for them, and re-layouts  60.1 us (7%)
  between operations  20.3 us (3%)
  starting transfers between devices  18.1 us (2%)
    another operation x30, other arithmetic, invert_factor(): factor = jnp.linalg.cholesky(block)  167 us
    psum x1, waiting for transfers between devices, on_device(): pivot_sum = lax.psum(pivot_partial, PAR)  148 us
    all_to_all x1, waiting for transfers between devices, on_device(): lax.all_to_all(jacobian, PAR, split_axis=1, concat_axis=0, tiled=True)  86.5 us
    another operation x3, other arithmetic, invert_factor(): lax.linalg.triangular_solve(factor, identity_matrix, left_side=True, lowe...  84.5 us
    another operation x15, matrix products, invert_factor(): lax.linalg.triangular_solve(factor, identity_matrix, left_side=True, lowe...  50.4 us
    reduce_scatter x1, waiting for transfers between devices, spread(): own = lax.psum_scatter(padded, axis, scatter_dimension=0, tiled=True)  39.4 us
    all_gather x1, waiting for transfers between devices, spread(): lax.all_gather(own, axis, axis=0, tiled=True)[:len(lines)]  35.3 us
    another operation x14, matrix products, invert_factor(): factor = jnp.linalg.cholesky(block)  25.9 us
  transfers between devices with their start and end apart: 7, of which 6 were waited for; matrix products, arithmetic and copies ran while one was open for 50% of the time, Pallas kernels for 0%

commit v1 on v0

v1 whole, which is shorter than its diff:
```python
import jax
import jax.numpy as jnp
from jax import lax
from jax.experimental import pallas as pl
from jax.experimental.pallas import tpu as pltpu
from jax.sharding import Mesh
from jax.sharding import PartitionSpec as P

PAR = ("z", "x")
PLANE = ("samp", "x")
ALL = ("samp", "z", "x")
NB = 128
HI = lax.Precision.HIGHEST


def rank_update(r):
    h = r.astype(jnp.bfloat16).astype(jnp.float32)
    m = (r - h).astype(jnp.bfloat16).astype(jnp.float32)
    l = (r - h - m).astype(jnp.bfloat16).astype(jnp.float32)
    lhs = jnp.concatenate([h, h, m, h, l, m], 0).astype(jnp.bfloat16)
    rhs = jnp.concatenate([h, m, h, l, h, m], 0).astype(jnp.bfloat16)
    return lax.dot_general(
        lhs, rhs, (((0,), (0,)), ((), ())), preferred_element_type=jnp.float32
    )


def inverse_of_factor(block):
    n = block.shape[0]
    groups = n // 8
    rows = [block[8 * i : 8 * i + 8, :] for i in range(groups)]
    sub = lax.broadcasted_iota(jnp.int32, (8, n), 0)
    lane = lax.broadcasted_iota(jnp.int32, (8, n), 1)
    for b in range(groups):
        r = rows[b]
        cols = [jnp.broadcast_to(r[:, 8 * b + j : 8 * b + j + 1], (8, n)) for j in range(8)]
        inside = (lane >= 8 * b) & (lane < 8 * b + 8)
        r = jnp.where(inside, jnp.where(lane == sub + 8 * b, 1.0, 0.0), r)
        diag = jnp.ones((8, n), jnp.float32)
        for j in range(8):
            d = jnp.broadcast_to(cols[j][j : j + 1, :], (8, n))
            diag = jnp.where(sub == j, d, diag)
            if j < 7:
                q = pl.reciprocal(d, approx=True)
                q = q * (2.0 - d * q)
                m = jnp.where(sub > j, cols[j] * q, 0.0)
                for c in range(j + 1, 8):
                    cols[c] = cols[c] - m * jnp.broadcast_to(cols[c][j : j + 1, :], (8, n))
                r = r - m * jnp.broadcast_to(r[j : j + 1, :], (8, n))
        s = lax.rsqrt(diag)
        s = s * (1.5 - 0.5 * diag * s * s)
        r = r * s
        rows[b] = r
        if b < groups - 1:
            p = rank_update(r)
            for i in range(b + 1, groups):
                rows[i] = jnp.where(inside, 0.0, rows[i]) - p[8 * i : 8 * i + 8, :]
    kept = [jnp.where(lane <= sub + 8 * b, rows[b], 0.0) for b in range(groups)]
    return jnp.concatenate(kept, 0)


def times_transposed(a, b):
    return lax.dot_general(
        a, b, (((1,), (1,)), ((), ())), precision=HI, preferred_element_type=jnp.float32
    )


def factor_kernel(a_ref, o_ref):
    n = a_ref.shape[0]
    steps = n // NB
    o_ref[...] = a_ref[...]
    for kb in range(steps):
        own = slice(kb * NB, kb * NB + NB)
        w = inverse_of_factor(o_ref[own, own])
        o_ref[own, own] = w
        if kb == steps - 1:
            break
        lo = (kb + 1) * NB
        o_ref[lo:, own] = times_transposed(o_ref[lo:, own], w)
        for j in range(kb + 1, steps):
            cj = slice(j * NB, j * NB + NB)
            o_ref[j * NB :, cj] = o_ref[j * NB :, cj] - times_transposed(
                o_ref[j * NB :, own], o_ref[cj, own]
            )


def factored(block):
    vmem = pl.BlockSpec(memory_space=pltpu.VMEM)
    n = block.shape[0]
    return pl.pallas_call(
        factor_kernel,
        out_shape=jax.ShapeDtypeStruct(block.shape, jnp.float32),
        in_specs=[vmem],
        out_specs=vmem,
        cost_estimate=pl.CostEstimate(flops=40 * n**3, bytes_accessed=8 * n * n, transcendentals=0),
        name="factor",
    )(block)


def solve_kernel(g_ref, f_ref, o_ref):
    n = f_ref.shape[0]
    o_ref[...] = g_ref[...]
    for kb in range(n // NB):
        own = slice(kb * NB, kb * NB + NB)
        x = times_transposed(o_ref[:, own], f_ref[own, own])
        o_ref[:, own] = x
        lo = (kb + 1) * NB
        if lo < n:
            o_ref[:, lo:] = o_ref[:, lo:] - times_transposed(x, f_ref[lo:, own])


def solved(rows, factor):
    vmem = pl.BlockSpec(memory_space=pltpu.VMEM)
    return pl.pallas_call(
        solve_kernel,
        out_shape=jax.ShapeDtypeStruct(rows.shape, jnp.float32),
        in_specs=[vmem, vmem],
        out_specs=vmem,
        name="solve",
    )(rows, factor)


def on_device(jacobian, sample_slot, panel_index, shift_value):
    width = sample_slot.shape[0]
    group_width = width * lax.axis_size(PAR)
    samples = group_width * lax.axis_size("samp")
    pivot_group = panel_index[0] // group_width
    rotation = panel_index[0] % group_width
    slots = lax.all_gather(sample_slot, ALL, axis=0, tiled=True)
    slots = slots.reshape(-1, group_width)
    own_slots = lax.dynamic_index_in_dim(slots, lax.axis_index("samp"), 0, keepdims=False)
    pivot_slots = lax.dynamic_index_in_dim(slots, pivot_group, 0, keepdims=False)
    column = jnp.arange(group_width, dtype=jnp.int32)
    chosen = (pivot_slots[None, :] == ((column + rotation) % group_width)[:, None]).astype(jnp.bfloat16)

    tile = lax.all_to_all(jacobian, PLANE, split_axis=1, concat_axis=0, tiled=True)
    band = group_width // lax.axis_size("z")
    mine = lax.dynamic_slice_in_dim(tile, pivot_group * band, band, 0)
    raw = lax.all_gather(mine, "z", axis=0, tiled=True)
    pivot = lax.dot_general(
        chosen, raw, (((1,), (0,)), ((), ())), preferred_element_type=jnp.float32
    ).astype(jnp.bfloat16)

    contract = (((1,), (1,)), ((), ()))
    part = lax.dynamic_slice_in_dim(pivot, lax.axis_index("z") * band, band, 0)
    pivot_part = lax.dot_general(part, pivot, contract, preferred_element_type=jnp.float32)
    pivot_share = lax.psum_scatter(pivot_part, PLANE, scatter_dimension=0, tiled=True)
    block = lax.all_gather(pivot_share, ("z", "samp", "x"), axis=0, tiled=True)
    identity_matrix = jnp.eye(group_width, dtype=jnp.float32)
    block = block / samples + shift_value[0] * identity_matrix

    partial = lax.dot_general(tile, pivot, contract, preferred_element_type=jnp.float32)
    rows = lax.psum_scatter(partial, PLANE, scatter_dimension=0, tiled=True)
    group_rows = lax.all_gather(rows, PAR, axis=0, tiled=True)
    position = lax.axis_index(PAR) * width + jnp.arange(width, dtype=jnp.int32)
    hit = own_slots[None, :] == position[:, None]
    source = jnp.sum(jnp.where(hit, column[None, :], 0), axis=1)
    my_rows = jnp.take(group_rows, source, axis=0) / samples
    on_pivot = lax.axis_index("samp") == pivot_group
    shifted = position[:, None] == ((column + rotation) % group_width)[None, :]
    my_rows = my_rows + jnp.where(shifted & on_pivot, shift_value[0], 0.0)
    return solved(my_rows, factored(block))


def solution(mesh):
    torus = Mesh(mesh.devices.reshape(mesh.shape["samp"], 8, 4), ("samp", "z", "x"))
    return jax.shard_map(
        on_device,
        mesh=torus,
        in_specs=(P(ALL, None), P(ALL), P(), P()),
        out_specs=P(ALL, None),
        check_vma=False,
    )
```

time: 806 us -> 589 us (0.73); the launches traced: 795 us -> 586 us
  other arithmetic: 274 us -> 11.1 us
  matrix products: 107 us -> 19.4 us
  blocking collectives: 0 us -> 82.1 us
  Pallas kernels: 0 us -> 69 us
  waiting for transfers between devices: 314 us -> 356 us
  local copies, waits for them, and re-layouts: 60.1 us -> 25.2 us
  starting transfers between devices: 18.1 us -> 8.01 us
    another operation x33 -> x0, other arithmetic: 252 us -> none  [the longest x30 167 us: invert_factor(): factor = jnp.linalg.cholesky(block)]
    psum x1 -> x0, waiting for transfers between devices: 148 us -> none  [on_device(): pivot_sum = lax.psum(pivot_partial, PAR)]
    unnamed x6, waiting for transfers between devices: 1.11 us -> 93.1 us
    all_gather x1 -> x3, waiting for transfers between devices: 35.3 us -> 122 us  [the longest x1 118 us: on_device(): block = lax.all_gather(pivot_share, ('z', 'samp', 'x'), axis=0, tiled=True)]
    unnamed x0 -> x1, blocking collectives: none -> 82.1 us
    another operation x29 -> x0, matrix products: 76.3 us -> none  [the longest x15 50.4 us: invert_factor(): lax.linalg.triangular_solve(factor, identity_matrix, left_side=True, lowe...]
    pallas_call x0 -> x2, Pallas kernels: none -> 69 us  [the longest x1 61.4 us: factored(): pl.pallas_call(factor_kernel, out_shape=jax.ShapeDtypeStruct(block.shape,...]
    reduce_scatter x2 -> x1, waiting for transfers between devices: 39.4 us -> 92.6 us  [on_device(): rows = lax.psum_scatter(partial, PLANE, scatter_dimension=0, tiled=True)]
  transfers between devices with their start and end apart: 7 -> 6, of which waited for: 6 -> 5; matrix products, arithmetic and copies ran while one was open for 50% -> 6% of each run, Pallas kernels for 0% -> 10%
where the time goes in v1:
time: 589 us; the launch traced here: 586 us
  waiting for transfers between devices  356 us (60%)
  blocking collectives  82.1 us (14%)
  Pallas kernels  69 us (12%)
  local copies, waits for them, and re-layouts  25.2 us (4%)
  matrix products  19.4 us (3%)
  between operations  15.3 us (3%)
  other arithmetic  11.1 us (2%)
  starting transfers between devices  8.01 us (1%)
    all_gather x1, waiting for transfers between devices, on_device(): block = lax.all_gather(pivot_share, ('z', 'samp', 'x'), axis=0, tiled=True)  118 us
    unnamed x6, waiting for transfers between devices  93.1 us
    reduce_scatter x1, waiting for transfers between devices, on_device(): rows = lax.psum_scatter(partial, PLANE, scatter_dimension=0, tiled=True)  92.6 us
    unnamed x1, blocking collectives  82.1 us
    pallas_call x1, Pallas kernels, factored(): pl.pallas_call(factor_kernel, out_shape=jax.ShapeDtypeStruct(block.shape,...  61.4 us
    all_to_all x1, waiting for transfers between devices, on_device(): lax.all_to_all(jacobian, PLANE, split_axis=1, concat_axis=0, tiled=True)  48.7 us
  transfers between devices with their start and end apart: 6, of which 5 were waited for; matrix products, arithmetic and copies ran while one was open for 6% of the time, Pallas kernels for 10%

profile of v1, /device:TPU:2, one launch (start us, length us, event | category | flops | bytes accessed | tf_op | source)
XLA Modules:
  0.0 586.3 jit_solution(6265451688131339567)
XLA Ops:
  6.5 4.7 copy.15
  11.3 7.8 %all-to-all-start = ((bf16[32,32,2048]{2,0,1:T(8,128)(2,1)}), bf16[32,32,2048]{2,0,1:T(8,128)(2,1)}, u32[]{:S(2)}, u32[]{:S(2)}) async-start(bf16[32,32,2048]{2,0,1:T(8,128)(2,1)} %bitcast.31), calls=%async_computation | async-start | bytes 8388608 | tf_op jit(solution)/shard_map/all_to_all | solution.py:135
  19.1 0.0 all-gather.5.cloned.1.call-start
  19.8 48.7 %all-to-all-done = bf16[32,32,2048]{2,0,1:T(8,128)(2,1)} async-done(((bf16[32,32,2048]{2,0,1:T(8,128)(2,1)}), bf16[32,32,2048]{2,0,1:T(8,128)(2,1)}, u32[]{:S(2)}, u32[]{:S(2)}) %all-to-all-start) | async-done | bytes 4194336 | tf_op jit(solution)/shard_map/all_to_all | solution.py:135
  68.5 1.9 constant_dynamic-slice_fusion
  70.5 0.0 all-reduce.4.cloned.1.call-start
  70.5 0.3 dynamic-update-slice
  70.8 82.1 %all-reduce = s32[8192]{0:T(1024)S(1)} all-reduce(s32[8192]{0:T(1024)S(1)} %dynamic-update-slice), channel_id=1, replica_groups=mesh['samp'=8,'z'=8,'x'=4] {'samp','z','x'}, use_global_device_ids=true, to_apply=%add | all-reduce | flops 8192 | bytes 65536
  153.0 0.0 all-gather.5.cloned.1.call-done
  153.0 7.1 %fusion.2 = bf16[1024,2048]{1,0:T(8,128)(2,1)S(1)} fusion(bf16[1024,2048]{1,0:T(8,128)(2,1)} %all-gather.5.cloned.1.call-done, s32[1024]{0:T(1024)S(1)} %bitcast.34, s32[1024]{0:T(1024)S(1)} %add_select_fusion), kind=kOutput, calls=%fused_computation.6 | convolution fusion | flops 4298113024 | bytes 8396800 | tf_op jit(solution)/shard_map/dot_general | solution.py:139
  160.1 2.0 copy-done
  162.1 2.3 fusion.7
  164.4 0.0 reduce-scatter.4.cloned.1.call-start
  164.5 10.1 %convolution_bitcast_fusion = f32[1024,1024]{0,1:T(8,128)} fusion(bf16[1024,2048]{1,0:T(8,128)(2,1)} %copy-done, bf16[1024,2048]{1,0:T(8,128)(2,1)} %bitcast.4), kind=kOutput, calls=%fused_computation.7 | convolution fusion | flops 4294967296 | bytes 12582912 | tf_op jit(solution)/shard_map/dot_general | solution.py:151
  174.6 5.5 copy.11
  180.0 0.0 all-gather.9.cloned.1.call-start
  180.1 0.6 copy-done.2
  180.7 0.6 dynamic-slice
  181.9 93.1 %all-reduce.4.cloned.1.call-done = f32[128,1024]{1,0:T(8,128)} async-done(((f32[128,1024]{1,0:T(8,128)}), f32[128,1024]{1,0:T(8,128)}) %all-reduce.4.cloned.1.call-update) | async-done | bytes 524304
  275.0 1.4 dynamic-slice_bitcast_fusion
  276.4 0.0 all-gather.7.cloned.1.call-start
  276.4 92.6 %reduce-scatter.4.cloned.1.call-done = f32[32,1024]{1,0:T(8,128)} async-done(((f32[1024,1024]{1,0:T(8,128)}), f32[32,1024]{1,0:T(8,128)}) %reduce-scatter.4.cloned.1.call-update) | async-done | bytes 131088 | tf_op jit(solution)/shard_map/reduce_scatter | solution.py:152
  369.7 0.2 select_reduce_fusion
  369.9 118.1 %all-gather.9.cloned.1.call-done = f32[256,4,1024]{2,1,0:T(4,128)} async-done(((f32[1,4,1024]{2,1,0:T(4,128)}), f32[256,4,1024]{2,1,0:T(4,128)}) %all-gather.9.cloned.1.call-update) | async-done | bytes 4194320 | tf_op jit(solution)/shard_map/all_gather | solution.py:147
  488.0 5.3 broadcast_multiply_fusion
  493.2 5.3 reshape.72
  498.5 4.9 select_add_fusion.a_ref
  503.4 61.4 %factor.1.f_ref = f32[1024,1024]{1,0:T(8,128)} custom-call(f32[1024,1024]{1,0:T(8,128)} %select_add_fusion.a_ref), custom_call_target="tpu_custom_call" | custom-call | flops 42949672960 | bytes 8388608 | tf_op jit(solution)/shard_map/factor/pallas_call | solution.py:89
  564.8 3.7 all-gather.7.cloned.1.call-done
  568.6 2.9 gather_fusion
  571.4 0.8 select_add_fusion.1.g_ref
  572.2 7.6 %solve.1 = f32[32,1024]{1,0:T(8,128)} custom-call(f32[32,1024]{1,0:T(8,128)} %select_add_fusion.1.g_ref, f32[1024,1024]{1,0:T(8,128)} %factor.1.f_ref), custom_call_target="tpu_custom_call" | custom-call | tf_op jit(solution)/shard_map/solve/pallas_call | solution.py:113
  (17 shorter events, 0.2 us)
Async XLA Ops:
  11.3 59.3 %copy-start.1 = (s32[32]{0:T(128)S(1)}, s32[32]{0:T(128)}, u32[]{:S(2)}) copy-start(s32[32]{0:T(128)} %param.5) | copy-start | bytes 388
  11.3 57.2 %all-to-all-start = ((bf16[32,32,2048]{2,0,1:T(8,128)(2,1)}), bf16[32,32,2048]{2,0,1:T(8,128)(2,1)}, u32[]{:S(2)}, u32[]{:S(2)}) async-start(bf16[32,32,2048]{2,0,1:T(8,128)(2,1)} %bitcast.31), calls=%async_computation | async-start | bytes 8388608 | tf_op jit(solution)/shard_map/all_to_all | solution.py:135
  19.1 133.9 %all-gather.5.cloned.1.call-start = ((), (), s32[]{:S(2)}) async-start(), calls=%async_computation.2 | async-start | bytes 4718592 | tf_op jit(solution)/shard_map/all_gather | solution.py:138
  70.5 204.5 %all-reduce.4.cloned.1.call-start = ((), (), s32[]{:S(2)}) async-start(), calls=%async_computation.6 | async-start | bytes 1048576
  160.1 2.0 copy-start
  164.4 204.6 %reduce-scatter.4.cloned.1.call-start = ((), (), s32[]{:S(2)}) async-start(), calls=%async_computation.5 | async-start | bytes 4325376 | tf_op jit(solution)/shard_map/reduce_scatter | solution.py:152
  180.0 0.7 copy-start.2
  180.0 307.9 %all-gather.9.cloned.1.call-start = ((), (), s32[]{:S(2)}) async-start(), calls=%async_computation.4 | async-start | bytes 4210688 | tf_op jit(solution)/shard_map/all_gather | solution.py:147
  276.4 292.2 %all-gather.7.cloned.1.call-start = ((), (), s32[]{:S(2)}) async-start(), calls=%async_computation.3 | async-start | bytes 4325376 | tf_op jit(solution)/shard_map/all_gather | solution.py:153
Sparse Core Ops, SparseCore 0:
  70.6 57.9 all-gather.4
  164.6 110.3 all-reduce.3
  278.9 90.0 reduce-scatter.3
  372.6 115.3 all-gather.8
  490.4 78.1 all-gather.6

commit v2 on v1

--- a/solution.py
+++ b/solution.py
@@ -119,23 +119,321 @@
     )(rows, factor)
 
 
+MESH_IDS = pl.DeviceIdType.MESH
+Z, X, Y, GROUPS = 8, 4, 4, 8
+
+
+def here():
+    samp, z, x = lax.axis_index("samp"), lax.axis_index("z"), lax.axis_index("x")
+    return samp, z, x
+
+
+def wrapped(value, size):
+    return lax.rem(value + size, size)
+
+
+def meet(peers):
+    barrier = pltpu.get_barrier_semaphore()
+    for peer in peers:
+        pl.semaphore_signal(barrier, inc=1, device_id=peer, device_id_type=MESH_IDS)
+    pl.semaphore_wait(barrier, len(peers))
+
+
+def at(samp, z, x):
+    return {"samp": samp, "z": z, "x": x}
+
+
+def plane_peers(samp, z, x):
+    return [
+        (ds, dx, at(wrapped(samp + ds, GROUPS), z, wrapped(x + dx, X)))
+        for ds in range(GROUPS)
+        for dx in range(X)
+        if (ds, dx) != (0, 0)
+    ]
+
+
+def column_peers(samp, z, x):
+    return [(dz, at(samp, wrapped(z + dz, Z), x)) for dz in range(1, Z)]
+
+
+def copy_to(src, dst, send, recv, peer):
+    return pltpu.make_async_remote_copy(
+        src_ref=src, dst_ref=dst, send_sem=send, recv_sem=recv,
+        device_id=peer, device_id_type=MESH_IDS,
+    )
+
+
+def pivots_kernel(mine_ref, slot_ref, out_ref, slots_ref, own_sem, send, recv, zs, zr, ps, pr):
+    samp, z, x = here()
+    right, left = wrapped(z + 1, Z), wrapped(z - 1, Z)
+    column, plane = column_peers(samp, z, x), plane_peers(samp, z, x)
+    meet([peer for _, peer in column] + [peer for _, _, peer in plane])
+    half = mine_ref.shape[0] // 2
+
+    sends = []
+    slots_ref[samp, z, x] = slot_ref[...]
+    for dz, peer in column:
+        sends.append(copy_to(slot_ref, slots_ref.at[samp, z, x], zs.at[dz], zr.at[dz], peer))
+        sends[-1].start()
+
+    own = pltpu.make_async_copy(mine_ref, out_ref.at[z], own_sem)
+    own.start()
+
+    def piece(owner, h):
+        return out_ref.at[owner, pl.ds(h * half, half)]
+
+    def arrival(d, s, h):
+        owner = wrapped(z - 1 - s, Z) if d == 0 else wrapped(z + 1 + s, Z)
+        ref = piece(owner, h)
+        return copy_to(ref, ref, send.at[d, s, h], recv.at[d, s, h], at(samp, z, x))
+
+    for s in range(4):
+        for h in range(2):
+            for d in range(2):
+                if s == 3 and h != d:
+                    continue
+                owner = wrapped(z - s, Z) if d == 0 else wrapped(z + s, Z)
+                if s > 0:
+                    arrival(d, s - 1, h).wait_recv()
+                source = mine_ref.at[pl.ds(h * half, half)] if s == 0 else piece(owner, h)
+                sends.append(
+                    copy_to(source, piece(owner, h), send.at[d, s, h], recv.at[d, s, h],
+                            at(samp, right if d == 0 else left, x))
+                )
+                sends[-1].start()
+        if s == 0:
+            for dz, _ in column:
+                ref = slots_ref.at[samp, wrapped(z - dz, Z), x]
+                copy_to(ref, ref, zs.at[dz], zr.at[dz], at(samp, z, x)).wait_recv()
+            for ds, dx, peer in plane:
+                ref = slots_ref.at[samp, :, x]
+                sends.append(copy_to(ref, ref, ps.at[ds, dx], pr.at[ds, dx], peer))
+                sends[-1].start()
+    for d in range(2):
+        for h in range(2):
+            for s in range(4):
+                if s == 3 and h == d or s == 2 and h != d:
+                    arrival(d, s, h).wait_recv()
+    for ds, dx, _ in plane:
+        ref = slots_ref.at[wrapped(samp - ds, GROUPS), :, wrapped(x - dx, X)]
+        copy_to(ref, ref, ps.at[ds, dx], pr.at[ds, dx], at(samp, z, x)).wait_recv()
+    for copy in sends:
+        copy.wait_send()
+    own.wait()
+
+
+def gathered_pivots(mine, slots):
+    vmem = pl.BlockSpec(memory_space=pltpu.VMEM)
+    dma = pltpu.SemaphoreType.DMA
+    band, width = mine.shape
+    return pl.pallas_call(
+        pivots_kernel,
+        out_shape=(
+            jax.ShapeDtypeStruct((Z, band, width), mine.dtype),
+            jax.ShapeDtypeStruct((GROUPS, Z, X, 1, 128), slots.dtype),
+        ),
+        in_specs=[vmem, vmem],
+        out_specs=(vmem, vmem),
+        scratch_shapes=[dma, dma((2, 4, 2)), dma((2, 4, 2)), dma((Z,)), dma((Z,)),
+                        dma((GROUPS, X)), dma((GROUPS, X))],
+        compiler_params=pltpu.CompilerParams(collective_id=0, has_side_effects=True),
+        name="gather_pivots",
+    )(mine, slots)
+
+
+def rows_kernel(c_ref, o_ref, sib, acc, first0, first1, acc0, acc1, second0, second1,
+                ss, sr, s0, r0, s1, r1, t0, q0, t1, q1):
+    samp, z, x = here()
+    y, core = samp // 2, lax.rem(samp, 2)
+    sibling = at(2 * y + 1 - core, z, x)
+    ring_y = [(d, wrapped(y + d, Y)) for d in range(1, Y)]
+    ring_x = [(d, wrapped(x + d, X)) for d in range(1, X)]
+    to_y = [at(2 * v + core, z, x) for _, v in ring_y]
+    to_x = [at(samp, z, v) for _, v in ring_x]
+    meet([sibling] + to_y + to_x)
+    wide = c_ref.shape[4] // 2
+    low, high = pl.ds(0, wide), pl.ds(wide, wide)
+    sends = []
+
+    def start(copy):
+        copy.start()
+        sends.append(copy)
+
+    order = (2, 1, 3, 0)
+    for d in order:
+        v = wrapped(y + d, Y)
+        start(copy_to(c_ref.at[v, 1 - core], sib.at[v], ss.at[d], sr.at[d], sibling))
+    for d in order:
+        v = wrapped(y + d, Y)
+        copy_to(sib.at[v], sib.at[v], ss.at[d], sr.at[d], sibling).wait_recv()
+        acc[v] = c_ref[v, core] + sib[v]
+        if d:
+            start(copy_to(acc.at[v, :, :, low], first0.at[d], s0.at[d], r0.at[d],
+                          at(2 * v + core, z, x)))
+    for d in (2, 1, 3):
+        u = wrapped(x + d, X)
+        start(copy_to(acc.at[:, u, :, high], first1.at[d], s1.at[d], r1.at[d], at(samp, z, u)))
+    me = at(samp, z, x)
+    for d in (1, 2, 3):
+        copy_to(first0.at[d], first0.at[d], s0.at[d], r0.at[d], me).wait_recv()
+    acc0[...] = acc[y, :, :, low] + first0[1] + first0[2] + first0[3]
+    for d in (2, 1, 3):
+        u = wrapped(x + d, X)
+        start(copy_to(acc0.at[u], second0.at[d], t0.at[d], q0.at[d], at(samp, z, u)))
+    for d in (1, 2, 3):
+        copy_to(first1.at[d], first1.at[d], s1.at[d], r1.at[d], me).wait_recv()
+    acc1[...] = acc[:, x, :, high] + first1[1] + first1[2] + first1[3]
+    for d in (2, 1, 3):
+        v = wrapped(y + d, Y)
+        start(copy_to(acc1.at[v], second1.at[d], t1.at[d], q1.at[d], at(2 * v + core, z, x)))
+    for d in (1, 2, 3):
+        copy_to(second0.at[d], second0.at[d], t0.at[d], q0.at[d], me).wait_recv()
+    o_ref[:, low] = acc0[x] + second0[1] + second0[2] + second0[3]
+    for d in (1, 2, 3):
+        copy_to(second1.at[d], second1.at[d], t1.at[d], q1.at[d], me).wait_recv()
+    o_ref[:, high] = acc1[y] + second1[1] + second1[2] + second1[3]
+    for copy in sends:
+        copy.wait_send()
+
+
+def summed_rows(partial):
+    vmem = pl.BlockSpec(memory_space=pltpu.VMEM)
+    dma = pltpu.SemaphoreType.DMA
+    n = partial.shape[1]
+    rows = partial.shape[0] // (GROUPS * X)
+    wide = n // 2
+    f32 = jnp.float32
+    return pl.pallas_call(
+        rows_kernel,
+        out_shape=jax.ShapeDtypeStruct((rows, n), f32),
+        in_specs=[vmem],
+        out_specs=vmem,
+        scratch_shapes=[
+            pltpu.VMEM((Y, X, rows, n), f32), pltpu.VMEM((Y, X, rows, n), f32),
+            pltpu.VMEM((Y, X, rows, wide), f32), pltpu.VMEM((X, Y, rows, wide), f32),
+            pltpu.VMEM((X, rows, wide), f32), pltpu.VMEM((Y, rows, wide), f32),
+            pltpu.VMEM((X, rows, wide), f32), pltpu.VMEM((Y, rows, wide), f32),
+        ] + [dma((4,))] * 10,
+        compiler_params=pltpu.CompilerParams(collective_id=1, has_side_effects=True),
+        name="sum_rows",
+    )(partial.reshape(Y, 2, X, rows, n))
+
+
+def block_kernel(p_ref, o_ref, got, piece, ps, pr, zs, zr, xs, xr, ys, yr, ys2, yr2, xs2, xr2, cs, cr):
+    samp, z, x = here()
+    y, core = samp // 2, lax.rem(samp, 2)
+    xh, xl = x // 2, lax.rem(x, 2)
+    sibling = at(2 * y + 1 - core, z, x)
+    column, plane = column_peers(samp, z, x), plane_peers(samp, z, x)
+    meet([peer for _, peer in column] + [peer for _, _, peer in plane])
+    me = at(samp, z, x)
+    wide = p_ref.shape[4] // 2
+    sends = []
+
+    def start(copy):
+        copy.start()
+        sends.append(copy)
+
+    def cols(xlow, color=None):
+        if color is None:
+            return pl.ds(pl.multiple_of(xlow * wide, wide), wide)
+        return pl.ds(pl.multiple_of(xlow * wide + color * (wide // 2), wide // 2), wide // 2)
+
+    def arrived(ref, send, recv):
+        copy_to(ref, ref, send, recv, me).wait_recv()
+
+    for ds, dx, peer in plane:
+        s, u = wrapped(samp + ds, GROUPS), wrapped(x + dx, X)
+        start(copy_to(p_ref.at[s // 2, lax.rem(s, 2), u // 2, :, cols(lax.rem(u, 2))],
+                      got.at[ds, dx], ps.at[ds, dx], pr.at[ds, dx], peer))
+    total = p_ref[y, core, xh, :, cols(xl)]
+    for ds, dx, _ in plane:
+        arrived(got.at[ds, dx], ps.at[ds, dx], pr.at[ds, dx])
+    for ds, dx, _ in plane:
+        total = total + got[ds, dx]
+    piece[...] = total
+    o_ref[z, y, core, xh, :, cols(xl)] = total
+    for dz, peer in column:
+        start(copy_to(piece, o_ref.at[z, y, core, xh, :, cols(xl)], zs.at[dz], zr.at[dz], peer))
+    for dz, _ in column:
+        arrived(o_ref.at[wrapped(z - dz, Z), y, core, xh, :, cols(xl)], zs.at[dz], zr.at[dz])
+    for d in (2, 1, 3):
+        v, u = wrapped(y + d, Y), wrapped(x + d, X)
+        ref0 = o_ref.at[:, y, core, xh, :, cols(xl, 0)]
+        start(copy_to(ref0, ref0, xs.at[d], xr.at[d], at(samp, z, u)))
+        ref1 = o_ref.at[:, y, core, xh, :, cols(xl, 1)]
+        start(copy_to(ref1, ref1, ys.at[d], yr.at[d], at(2 * v + core, z, x)))
+    for d in (1, 2, 3):
+        u = wrapped(x - d, X)
+        arrived(o_ref.at[:, y, core, u // 2, :, cols(lax.rem(u, 2), 0)], xs.at[d], xr.at[d])
+    for d in (2, 1, 3):
+        v = wrapped(y + d, Y)
+        for low in range(2):
+            ref = o_ref.at[:, y, core, :, :, cols(low, 0)]
+            start(copy_to(ref, ref, ys2.at[d, low], yr2.at[d, low], at(2 * v + core, z, x)))
+    for d in (1, 2, 3):
+        v = wrapped(y - d, Y)
+        arrived(o_ref.at[:, v, core, xh, :, cols(xl, 1)], ys.at[d], yr.at[d])
+    for d in (2, 1, 3):
+        u = wrapped(x + d, X)
+        ref = o_ref.at[:, :, core, xh, :, cols(xl, 1)]
+        start(copy_to(ref, ref, xs2.at[d], xr2.at[d], at(samp, z, u)))
+    for d in (1, 3, 2):
+        v = wrapped(y - d, Y)
+        for low in range(2):
+            arrived(o_ref.at[:, v, core, :, :, cols(low, 0)], ys2.at[d, low], yr2.at[d, low])
+    for d in (1, 3, 2):
+        u = wrapped(x - d, X)
+        arrived(o_ref.at[:, :, core, u // 2, :, cols(lax.rem(u, 2), 1)], xs2.at[d], xr2.at[d])
+    for v in range(Y):
+        ref = o_ref.at[:, v, core]
+        start(copy_to(ref, ref, cs.at[v], cr.at[v], sibling))
+    for v in range(Y):
+        arrived(o_ref.at[:, v, 1 - core], cs.at[v], cr.at[v])
+    for copy in sends:
+        copy.wait_send()
+
+
+def summed_block(part):
+    vmem = pl.BlockSpec(memory_space=pltpu.VMEM)
+    dma = pltpu.SemaphoreType.DMA
+    band, n = part.shape
+    f32 = jnp.float32
+    out = pl.pallas_call(
+        block_kernel,
+        out_shape=jax.ShapeDtypeStruct((Z, Y, 2, 2, 8, n), f32),
+        in_specs=[vmem],
+        out_specs=vmem,
+        scratch_shapes=[
+            pltpu.VMEM((GROUPS, X, 8, n // 2), f32), pltpu.VMEM((8, n // 2), f32),
+            dma((GROUPS, X)), dma((GROUPS, X)), dma((Z,)), dma((Z,)),
+            dma((4,)), dma((4,)), dma((4,)), dma((4,)),
+            dma((4, 2)), dma((4, 2)), dma((4,)), dma((4,)), dma((4,)), dma((4,)),
+        ],
+        compiler_params=pltpu.CompilerParams(collective_id=2, has_side_effects=True),
+        name="sum_block",
+    )(part.reshape(Y, 2, 2, 8, n))
+    return out.reshape(Z * band, n)
+
+
 def on_device(jacobian, sample_slot, panel_index, shift_value):
     width = sample_slot.shape[0]
     group_width = width * lax.axis_size(PAR)
     samples = group_width * lax.axis_size("samp")
     pivot_group = panel_index[0] // group_width
     rotation = panel_index[0] % group_width
-    slots = lax.all_gather(sample_slot, ALL, axis=0, tiled=True)
-    slots = slots.reshape(-1, group_width)
+    tile = lax.all_to_all(jacobian, PLANE, split_axis=1, concat_axis=0, tiled=True)
+    band = group_width // lax.axis_size("z")
+    mine = lax.dynamic_slice_in_dim(tile, pivot_group * band, band, 0)
+    padded = jnp.pad(sample_slot, (0, 128 - width)).reshape(1, 128)
+    raw, slots = gathered_pivots(mine, padded)
+    raw = raw.reshape(group_width, -1)
+    slots = slots[..., 0, :width].reshape(-1, group_width)
     own_slots = lax.dynamic_index_in_dim(slots, lax.axis_index("samp"), 0, keepdims=False)
     pivot_slots = lax.dynamic_index_in_dim(slots, pivot_group, 0, keepdims=False)
     column = jnp.arange(group_width, dtype=jnp.int32)
     chosen = (pivot_slots[None, :] == ((column + rotation) % group_width)[:, None]).astype(jnp.bfloat16)
 
-    tile = lax.all_to_all(jacobian, PLANE, split_axis=1, concat_axis=0, tiled=True)
-    band = group_width // lax.axis_size("z")
-    mine = lax.dynamic_slice_in_dim(tile, pivot_group * band, band, 0)
-    raw = lax.all_gather(mine, "z", axis=0, tiled=True)
     pivot = lax.dot_general(
         chosen, raw, (((1,), (0,)), ((), ())), preferred_element_type=jnp.float32
     ).astype(jnp.bfloat16)
@@ -143,14 +441,13 @@
     contract = (((1,), (1,)), ((), ()))
     part = lax.dynamic_slice_in_dim(pivot, lax.axis_index("z") * band, band, 0)
     pivot_part = lax.dot_general(part, pivot, contract, preferred_element_type=jnp.float32)
-    pivot_share = lax.psum_scatter(pivot_part, PLANE, scatter_dimension=0, tiled=True)
-    block = lax.all_gather(pivot_share, ("z", "samp", "x"), axis=0, tiled=True)
+    partial = lax.dot_general(tile, pivot, contract, preferred_element_type=jnp.float32)
+    rows = summed_rows(partial)
+    group_rows = lax.all_gather(rows, PAR, axis=0, tiled=True)
+    block = summed_block(pivot_part)
     identity_matrix = jnp.eye(group_width, dtype=jnp.float32)
     block = block / samples + shift_value[0] * identity_matrix
 
-    partial = lax.dot_general(tile, pivot, contract, preferred_element_type=jnp.float32)
-    rows = lax.psum_scatter(partial, PLANE, scatter_dimension=0, tiled=True)
-    group_rows = lax.all_gather(rows, PAR, axis=0, tiled=True)
     position = lax.axis_index(PAR) * width + jnp.arange(width, dtype=jnp.int32)
     hit = own_slots[None, :] == position[:, None]
     source = jnp.sum(jnp.where(hit, column[None, :], 0), axis=1)

time: 589 us -> 309 us (0.52)
  waiting for transfers between devices: 356 us -> 48.1 us
  Pallas kernels: 69 us -> 197 us
  blocking collectives: 82.1 us -> 0 us
  local copies, waits for them, and re-layouts: 25.2 us -> 11.5 us
    pallas_call x0 -> x3, Pallas kernels: none -> 128 us  [the longest x1 54.6 us: gathered_pivots(): pl.pallas_call(pivots_kernel, out_shape=(jax.ShapeDtypeStruct((Z, band, w...]
    all_gather x2 -> x0, waiting for transfers between devices: 118 us -> none  [the longest x1 118 us: on_device(): block = lax.all_gather(pivot_share, ('z', 'samp', 'x'), axis=0, tiled=True)]
    unnamed x6 -> x1, waiting for transfers between devices: 93.1 us -> 0.02 us
    reduce_scatter x1 -> x0, waiting for transfers between devices: 92.6 us -> none  [on_device(): rows = lax.psum_scatter(partial, PLANE, scatter_dimension=0, tiled=True)]
    unnamed x1 -> x0, blocking collectives: 82.1 us -> none
    unnamed x11 -> x4, local copies, waits for them, and re-layouts: 10.3 us -> 0.01 us
  transfers between devices with their start and end apart: 6 -> 2, of which waited for: 5 -> 1; matrix products, arithmetic and copies ran while one was open for 6% -> 3% of each run, Pallas kernels for 10% -> 35%
where the time goes in v2:
time: 309 us; the launch traced here: 307 us
  Pallas kernels  197 us (64%)
  waiting for transfers between devices  48.1 us (16%)
  matrix products  21.6 us (7%)
  between operations  14.9 us (5%)
  local copies, waits for them, and re-layouts  11.5 us (4%)
  starting transfers between devices  7.85 us (3%)
  other arithmetic  5.84 us (2%)
    pallas_call x1, Pallas kernels, factored(): pl.pallas_call(factor_kernel, out_shape=jax.ShapeDtypeStruct(block.shape,...  61.6 us
    pallas_call x1, Pallas kernels, gathered_pivots(): pl.pallas_call(pivots_kernel, out_shape=(jax.ShapeDtypeStruct((Z, band, w...  54.6 us
    all_to_all x1, waiting for transfers between devices, on_device(): lax.all_to_all(jacobian, PLANE, split_axis=1, concat_axis=0, tiled=True)  48.1 us
    pallas_call x1, Pallas kernels, summed_block(): pl.pallas_call(block_kernel, out_shape=jax.ShapeDtypeStruct((Z, Y, 2, 2,...  45.1 us
    pallas_call x1, Pallas kernels, summed_rows(): pl.pallas_call(rows_kernel, out_shape=jax.ShapeDtypeStruct((rows, n), f32...  27.8 us
    dot_general x1, matrix products, on_device(): lax.dot_general(tile, pivot, contract, preferred_element_type=jnp.float32)  9.8 us
    all_to_all x1, starting transfers between devices, on_device(): lax.all_to_all(jacobian, PLANE, split_axis=1, concat_axis=0, tiled=True)  7.8 us
    pallas_call x1, Pallas kernels, solved(): pl.pallas_call(solve_kernel, out_shape=jax.ShapeDtypeStruct(rows.shape, j...  7.6 us
  transfers between devices with their start and end apart: 2, of which 1 were waited for; matrix products, arithmetic and copies ran while one was open for 3% of the time, Pallas kernels for 35%

profile of v2, /device:TPU:2, one launch (start us, length us, event | category | flops | bytes accessed | tf_op | source)
XLA Modules:
  0.0 306.5 jit_solution(7252627444405400572)
XLA Ops:
  6.5 4.7 %copy.8 = bf16[4,32,8,2048]{3,2,0,1:T(8,128)(2,1)} copy(bf16[4,32,8,2048]{3,2,1,0:T(8,128)(2,1)} %bitcast.35) | data formatting | bytes 8388608 | tf_op jit(solution)/shard_map/all_to_all | solution.py:425
  11.3 0.0 copy-start.1
  11.3 7.8 %all-to-all-start = ((bf16[32,32,2048]{2,0,1:T(8,128)(2,1)}), bf16[32,32,2048]{2,0,1:T(8,128)(2,1)}, u32[]{:S(2)}, u32[]{:S(2)}) async-start(bf16[32,32,2048]{2,0,1:T(8,128)(2,1)} %bitcast.34), calls=%async_computation | async-start | bytes 8388608 | tf_op jit(solution)/shard_map/all_to_all | solution.py:425
  19.1 0.0 all-gather.2.cloned.1.call-start
  19.8 0.0 copy-done.1
  19.8 0.5 pad_bitcast_fusion.slot_ref
  20.4 48.1 %all-to-all-done = bf16[32,32,2048]{2,0,1:T(8,128)(2,1)} async-done(((bf16[32,32,2048]{2,0,1:T(8,128)(2,1)}), bf16[32,32,2048]{2,0,1:T(8,128)(2,1)}, u32[]{:S(2)}, u32[]{:S(2)}) %all-to-all-start) | async-done | bytes 4194336 | tf_op jit(solution)/shard_map/all_to_all | solution.py:425
  68.5 1.9 constant_dynamic-slice_fusion.2.mine_ref
  70.4 54.6 %gather_pivots.1 = (bf16[8,128,2048]{2,1,0:T(8,128)(2,1)}, s32[8,8,4,1,128]{4,3,2,1,0:T(1,128)}) custom-call(bf16[128,2048]{1,0:T(8,128)(2,1)} %constant_dynamic-slice_fusion.2.mine_ref, s32[1,128]{1,0:T(1,128)} %pad_bitcast_fusion.slot_ref), custom_call_target="tpu_custom_call" | custom-call | tf_op jit(solution)/shard_map/gather_pivots/pallas_call | solution.py:229
  125.1 1.3 slice_reduce_fusion
  126.3 0.1 reshape_squeeze.3
  126.5 7.1 %fusion.2 = bf16[1024,2048]{1,0:T(8,128)(2,1)S(1)} fusion(bf16[1024,2048]{1,0:T(8,128)(2,1)} %bitcast.40, s32[1024]{0:T(1024)S(1)} %bitcast.39, s32[1024]{0:T(1024)S(1)} %add_select_fusion), kind=kOutput, calls=%fused_computation.6 | convolution fusion | flops 4298113024 | bytes 8396800 | tf_op jit(solution)/shard_map/dot_general | solution.py:437
  133.6 0.0 copy-start
  133.6 9.8 %fusion.15 = f32[1024,1024]{0,1:T(8,128)} fusion(bf16[1024,2048]{1,0:T(8,128)(2,1)S(1)} %fusion.2, bf16[1024,2048]{1,0:T(8,128)(2,1)} %bitcast.1), kind=kOutput, calls=%fused_computation.33 | convolution fusion | flops 4294967296 | bytes 12582912 | tf_op jit(solution)/shard_map/dot_general | solution.py:444
  143.4 0.0 copy-done
  143.4 27.8 %sum_rows.1 = f32[32,1024]{1,0:T(8,128)} custom-call(f32[4,2,4,32,1024]{4,3,2,1,0:T(8,128)} %bitcast.36), custom_call_target="tpu_custom_call" | custom-call | tf_op jit(solution)/shard_map/sum_rows/pallas_call | solution.py:306
  171.2 0.0 all-gather.2.cloned.1.call-update
  171.9 4.7 %fusion.7 = f32[128,1024]{1,0:T(8,128)} fusion(bf16[1024,2048]{1,0:T(8,128)(2,1)} %copy-done, s32[]{:T(128)S(6)} %select_n.79), kind=kOutput, calls=%fused_computation.10 | convolution fusion | flops 536870912 | bytes 5242884 | tf_op jit(solution)/shard_map/dot_general | solution.py:443
  176.6 45.1 %sum_block.1 = f32[8,4,2,2,8,1024]{5,4,3,2,1,0:T(8,128)} custom-call(f32[4,2,2,8,1024]{4,3,2,1,0:T(8,128)} %bitcast.37), custom_call_target="tpu_custom_call" | custom-call | tf_op jit(solution)/shard_map/sum_block/pallas_call | solution.py:402
  221.7 0.2 select_reduce_fusion
  222.0 2.6 broadcast_multiply_fusion
  224.6 2.2 bitcast_add_fusion.a_ref
  226.8 61.6 %factor.1.f_ref = f32[1024,1024]{1,0:T(8,128)} custom-call(f32[1024,1024]{1,0:T(8,128)} %bitcast_add_fusion.a_ref), custom_call_target="tpu_custom_call" | custom-call | flops 42949672960 | bytes 8388608 | tf_op jit(solution)/shard_map/factor/pallas_call | solution.py:89
  288.4 0.0 all-gather.2.cloned.1.call-done
  288.4 2.9 gather_fusion
  291.3 0.8 select_add_fusion.g_ref
  292.1 7.6 %solve.1 = f32[32,1024]{1,0:T(8,128)} custom-call(f32[32,1024]{1,0:T(8,128)} %select_add_fusion.g_ref, f32[1024,1024]{1,0:T(8,128)} %factor.1.f_ref), custom_call_target="tpu_custom_call" | custom-call | tf_op jit(solution)/shard_map/solve/pallas_call | solution.py:113
  (6 shorter events, 0.1 us)
Async XLA Ops:
  11.3 8.6 %copy-start.1 = (s32[32]{0:T(128)S(1)}, s32[32]{0:T(128)}, u32[]{:S(2)}) copy-start(s32[32]{0:T(128)} %param.5) | copy-start | bytes 388
  11.3 57.2 %all-to-all-start = ((bf16[32,32,2048]{2,0,1:T(8,128)(2,1)}), bf16[32,32,2048]{2,0,1:T(8,128)(2,1)}, u32[]{:S(2)}, u32[]{:S(2)}) async-start(bf16[32,32,2048]{2,0,1:T(8,128)(2,1)} %bitcast.34), calls=%async_computation | async-start | bytes 8388608 | tf_op jit(solution)/shard_map/all_to_all | solution.py:425
  19.1 269.4 %all-gather.2.cloned.1.call-start = ((), (), s32[]{:S(2)}) async-start(), calls=%async_computation.1 | async-start | bytes 4325376 | tf_op jit(solution)/shard_map/all_gather | solution.py:446
  133.6 9.8 %copy-start = (bf16[1024,2048]{1,0:T(8,128)(2,1)}, bf16[1024,2048]{1,0:T(8,128)(2,1)S(1)}, u32[]{:S(2)}) copy-start(bf16[1024,2048]{1,0:T(8,128)(2,1)S(1)} %fusion.2) | copy-start | bytes 12582916
Sparse Core Ops, SparseCore 0:
  171.4 78.2 all-gather.1

commit v3 on v2

--- a/solution.py
+++ b/solution.py
@@ -121,6 +121,7 @@
 
 MESH_IDS = pl.DeviceIdType.MESH
 Z, X, Y, GROUPS = 8, 4, 4, 8
+CHUNKS = 4
 
 
 def here():
@@ -163,82 +164,114 @@
     )
 
 
-def pivots_kernel(mine_ref, slot_ref, out_ref, slots_ref, own_sem, send, recv, zs, zr, ps, pr):
+def exchange_kernel(jac_ref, slot_ref, group_ref, tile_ref, pivot_ref, slots_ref,
+                    own_sem, send, recv, zsend, zrecv, ps, pr, zs, zr):
     samp, z, x = here()
     right, left = wrapped(z + 1, Z), wrapped(z - 1, Z)
     column, plane = column_peers(samp, z, x), plane_peers(samp, z, x)
+    me = at(samp, z, x)
     meet([peer for _, peer in column] + [peer for _, _, peer in plane])
-    half = mine_ref.shape[0] // 2
-
+    rows = jac_ref.shape[0]
+    tile = tile_ref.shape[-1]
+    wide = tile // CHUNKS
     sends = []
+
+    def start(copy):
+        copy.start()
+        sends.append(copy)
+
+    def arrived(ref, send_sem, recv_sem):
+        copy_to(ref, ref, send_sem, recv_sem, me).wait_recv()
+
+    def cols(q):
+        return pl.ds(q * wide, wide)
+
     slots_ref[samp, z, x] = slot_ref[...]
+    for ds, dx, peer in plane:
+        start(copy_to(slot_ref, slots_ref.at[samp, z, x], ps.at[ds, dx], pr.at[ds, dx], peer))
+
+    owns = []
+    for q in range(CHUNKS):
+        for ds, dx, peer in plane:
+            s, u = wrapped(samp + ds, GROUPS), wrapped(x + dx, X)
+            first = pl.multiple_of((s * X + u) * tile + q * wide, wide)
+            start(copy_to(jac_ref.at[:, pl.ds(first, wide)], tile_ref.at[samp, x, :, cols(q)],
+                          send.at[q, ds, dx], recv.at[q, ds, dx], peer))
+        first = pl.multiple_of((samp * X + x) * tile + q * wide, wide)
+        owns.append(pltpu.make_async_copy(jac_ref.at[:, pl.ds(first, wide)],
+                                          tile_ref.at[samp, x, :, cols(q)], own_sem.at[q]))
+        owns[-1].start()
+
+    for ds, dx, _ in plane:
+        arrived(slots_ref.at[wrapped(samp - ds, GROUPS), z, wrapped(x - dx, X)],
+                ps.at[ds, dx], pr.at[ds, dx])
     for dz, peer in column:
-        sends.append(copy_to(slot_ref, slots_ref.at[samp, z, x], zs.at[dz], zr.at[dz], peer))
-        sends[-1].start()
-
-    own = pltpu.make_async_copy(mine_ref, out_ref.at[z], own_sem)
-    own.start()
-
-    def piece(owner, h):
-        return out_ref.at[owner, pl.ds(h * half, half)]
-
-    def arrival(d, s, h):
+        ref = slots_ref.at[:, z]
+        start(copy_to(ref, ref, zs.at[dz], zr.at[dz], peer))
+
+    def hop(d, s, q):
+        owner = wrapped(z - s, Z) if d == 0 else wrapped(z + s, Z)
+        ref = pivot_ref.at[owner, :, :, cols(q)]
+        start(copy_to(ref, ref, zsend.at[d, s, q], zrecv.at[d, s, q],
+                      at(samp, right if d == 0 else left, x)))
+
+    def came(d, s, q):
         owner = wrapped(z - 1 - s, Z) if d == 0 else wrapped(z + 1 + s, Z)
-        ref = piece(owner, h)
-        return copy_to(ref, ref, send.at[d, s, h], recv.at[d, s, h], at(samp, z, x))
-
-    for s in range(4):
-        for h in range(2):
+        arrived(pivot_ref.at[owner, :, :, cols(q)], zsend.at[d, s, q], zrecv.at[d, s, q])
+
+    def farthest(d, q):
+        return d == q % 2
+
+    def forward(q):
+        for s in range(1, 4):
             for d in range(2):
-                if s == 3 and h != d:
-                    continue
-                owner = wrapped(z - s, Z) if d == 0 else wrapped(z + s, Z)
-                if s > 0:
-                    arrival(d, s - 1, h).wait_recv()
-                source = mine_ref.at[pl.ds(h * half, half)] if s == 0 else piece(owner, h)
-                sends.append(
-                    copy_to(source, piece(owner, h), send.at[d, s, h], recv.at[d, s, h],
-                            at(samp, right if d == 0 else left, x))
-                )
-                sends[-1].start()
-        if s == 0:
-            for dz, _ in column:
-                ref = slots_ref.at[samp, wrapped(z - dz, Z), x]
-                copy_to(ref, ref, zs.at[dz], zr.at[dz], at(samp, z, x)).wait_recv()
-            for ds, dx, peer in plane:
-                ref = slots_ref.at[samp, :, x]
-                sends.append(copy_to(ref, ref, ps.at[ds, dx], pr.at[ds, dx], peer))
-                sends[-1].start()
-    for d in range(2):
-        for h in range(2):
-            for s in range(4):
-                if s == 3 and h == d or s == 2 and h != d:
-                    arrival(d, s, h).wait_recv()
-    for ds, dx, _ in plane:
-        ref = slots_ref.at[wrapped(samp - ds, GROUPS), :, wrapped(x - dx, X)]
-        copy_to(ref, ref, ps.at[ds, dx], pr.at[ds, dx], at(samp, z, x)).wait_recv()
+                came(d, s - 1, q)
+                if s < 3 or farthest(d, q):
+                    hop(d, s, q)
+
+    for q in range(CHUNKS):
+        for ds, dx, _ in plane:
+            arrived(tile_ref.at[wrapped(samp - ds, GROUPS), wrapped(x - dx, X), :, cols(q)],
+                    send.at[q, ds, dx], recv.at[q, ds, dx])
+        owns[q].wait()
+        picked = tile_ref[0, :, :, cols(q)]
+        for g in range(1, GROUPS):
+            picked = jnp.where(group_ref[0] == g, tile_ref[g, :, :, cols(q)], picked)
+        pivot_ref[z, :, :, cols(q)] = picked
+        for d in range(2):
+            hop(d, 0, q)
+        if q > 0:
+            forward(q - 1)
+    forward(CHUNKS - 1)
+    for q in range(CHUNKS):
+        came(0 if farthest(0, q) else 1, 3, q)
+    for dz, _ in column:
+        arrived(slots_ref.at[:, wrapped(z - dz, Z)], zs.at[dz], zr.at[dz])
     for copy in sends:
         copy.wait_send()
-    own.wait()
-
-
-def gathered_pivots(mine, slots):
+
+
+def exchanged(jacobian, slots, group):
     vmem = pl.BlockSpec(memory_space=pltpu.VMEM)
     dma = pltpu.SemaphoreType.DMA
-    band, width = mine.shape
+    rows, params = jacobian.shape
+    tile = params // (GROUPS * X)
     return pl.pallas_call(
-        pivots_kernel,
+        exchange_kernel,
         out_shape=(
-            jax.ShapeDtypeStruct((Z, band, width), mine.dtype),
+            jax.ShapeDtypeStruct((GROUPS, X, rows, tile), jacobian.dtype),
+            jax.ShapeDtypeStruct((Z, X, rows, tile), jacobian.dtype),
             jax.ShapeDtypeStruct((GROUPS, Z, X, 1, 128), slots.dtype),
         ),
-        in_specs=[vmem, vmem],
-        out_specs=(vmem, vmem),
-        scratch_shapes=[dma, dma((2, 4, 2)), dma((2, 4, 2)), dma((Z,)), dma((Z,)),
-                        dma((GROUPS, X)), dma((GROUPS, X))],
+        in_specs=[pl.BlockSpec(memory_space=pl.ANY), vmem,
+                  pl.BlockSpec(memory_space=pltpu.SMEM)],
+        out_specs=(vmem, vmem, vmem),
+        scratch_shapes=[dma((CHUNKS,)), dma((CHUNKS, GROUPS, X)), dma((CHUNKS, GROUPS, X)),
+                        dma((2, 4, CHUNKS)), dma((2, 4, CHUNKS)),
+                        dma((GROUPS, X)), dma((GROUPS, X)), dma((Z,)), dma((Z,))],
         compiler_params=pltpu.CompilerParams(collective_id=0, has_side_effects=True),
-        name="gather_pivots",
-    )(mine, slots)
+        name="exchange",
+    )(jacobian, slots, group)
 
 
 def rows_kernel(c_ref, o_ref, sib, acc, first0, first1, acc0, acc1, second0, second1,
@@ -422,11 +455,10 @@
     samples = group_width * lax.axis_size("samp")
     pivot_group = panel_index[0] // group_width
     rotation = panel_index[0] % group_width
-    tile = lax.all_to_all(jacobian, PLANE, split_axis=1, concat_axis=0, tiled=True)
     band = group_width // lax.axis_size("z")
-    mine = lax.dynamic_slice_in_dim(tile, pivot_group * band, band, 0)
     padded = jnp.pad(sample_slot, (0, 128 - width)).reshape(1, 128)
-    raw, slots = gathered_pivots(mine, padded)
+    tile, raw, slots = exchanged(jacobian, padded, pivot_group.reshape(1))
+    tile = tile.reshape(group_width, -1)
     raw = raw.reshape(group_width, -1)
     slots = slots[..., 0, :width].reshape(-1, group_width)
     own_slots = lax.dynamic_index_in_dim(slots, lax.axis_index("samp"), 0, keepdims=False)

time: 309 us -> 291 us (0.942)
  waiting for transfers between devices: 48.1 us -> 0.02 us
  Pallas kernels: 197 us -> 242 us
  starting transfers between devices: 7.85 us -> 0.01 us
  local copies, waits for them, and re-layouts: 11.5 us -> 7.41 us
  matrix products: 21.6 us -> 18 us
    all_to_all x1 -> x0, waiting for transfers between devices: 48.1 us -> none  [on_device(): lax.all_to_all(jacobian, PLANE, split_axis=1, concat_axis=0, tiled=True)]
    pallas_call x1, Pallas kernels: 54.6 us -> 98 us  [exchanged(): pl.pallas_call(exchange_kernel, out_shape=(jax.ShapeDtypeStruct((GROUPS,...]
    all_to_all x1 -> x0, starting transfers between devices: 7.8 us -> none  [on_device(): lax.all_to_all(jacobian, PLANE, split_axis=1, concat_axis=0, tiled=True)]
    all_to_all x1 -> x0, local copies, waits for them, and re-layouts: 4.74 us -> none  [on_device(): lax.all_to_all(jacobian, PLANE, split_axis=1, concat_axis=0, tiled=True)]
    dot_general x1, matrix products: 9.8 us -> 6.09 us  [on_device(): lax.dot_general(tile, pivot, contract, preferred_element_type=jnp.float32)]
  transfers between devices with their start and end apart: 2 -> 1, of which waited for: 1 -> 0; matrix products, arithmetic and copies ran while one was open for 3% -> 3% of each run, Pallas kernels for 35% -> 38%
where the time goes in v3:
time: 291 us; the launch traced here: 288 us
  Pallas kernels  242 us (83%)
  matrix products  18 us (6%)
  between operations  14.8 us (5%)
  local copies, waits for them, and re-layouts  7.41 us (3%)
  other arithmetic  5.86 us (2%)
    pallas_call x1, Pallas kernels, exchanged(): pl.pallas_call(exchange_kernel, out_shape=(jax.ShapeDtypeStruct((GROUPS,...  98 us
    pallas_call x1, Pallas kernels, factored(): pl.pallas_call(factor_kernel, out_shape=jax.ShapeDtypeStruct(block.shape,...  61.6 us
    pallas_call x1, Pallas kernels, summed_block(): pl.pallas_call(block_kernel, out_shape=jax.ShapeDtypeStruct((Z, Y, 2, 2,...  46.6 us
    pallas_call x1, Pallas kernels, summed_rows(): pl.pallas_call(rows_kernel, out_shape=jax.ShapeDtypeStruct((rows, n), f32...  28.2 us
    pallas_call x1, Pallas kernels, solved(): pl.pallas_call(solve_kernel, out_shape=jax.ShapeDtypeStruct(rows.shape, j...  7.6 us
    dot_general x1, matrix products, on_device(): lax.dot_general(chosen, raw, (((1,), (0,)), ((), ())), preferred_element_...  7.22 us
    dot_general x1, matrix products, on_device(): lax.dot_general(tile, pivot, contract, preferred_element_type=jnp.float32)  6.09 us
  transfers between devices with their start and end apart: 1, of which 0 were waited for; matrix products, arithmetic and copies ran while one was open for 3% of the time, Pallas kernels for 38%

profile of v3, /device:TPU:2, one launch (start us, length us, event | category | flops | bytes accessed | tf_op | source)
XLA Modules:
  0.0 288.2 jit_solution(10672811331550932110)
XLA Ops:
  6.5 0.0 all-gather.2.cloned.1.call-start
  7.2 1.2 pad_bitcast_fusion.slot_ref
  8.4 98.0 %exchange.1 = (bf16[8,4,32,2048]{3,2,1,0:T(8,128)(2,1)}, bf16[8,4,32,2048]{3,2,1,0:T(8,128)(2,1)}, s32[8,8,4,1,128]{4,3,2,1,0:T(1,128)}) custom-call(bf16[32,65536]{1,0:T(8,128)(2,1)} %jac_ref.1, s32[1,128]{1,0:T(1,128)} %pad_bitcast_fusion.slot_ref, s32[1]{0:T(128)} %bitcast.2.group_ref), custom_call_target="tpu_custom_call" | custom-call | tf_op jit(solution)/shard_map/exchange/pallas_call | solution.py:259
  106.4 1.3 slice_reduce_fusion
  107.7 0.1 reshape_squeeze.3
  107.9 0.0 copy-start.1
  107.9 7.2 %fusion.4 = bf16[1024,2048]{1,0:T(8,128)(2,1)S(1)} fusion(bf16[1024,2048]{1,0:T(8,128)(2,1)} %bitcast.34, s32[1024]{0:T(1024)S(1)} %bitcast.32, s32[1024]{0:T(1024)S(1)} %add_select_fusion), kind=kOutput, calls=%fused_computation.7 | convolution fusion | flops 4298113024 | bytes 8396800 | tf_op jit(solution)/shard_map/dot_general | solution.py:469
  115.1 0.0 copy-start
  115.1 2.0 copy-done
  117.1 0.0 copy-done.1
  117.1 6.1 %fusion.c_ref = f32[4,2,4,32,1024]{4,3,2,1,0:T(8,128)} fusion(bf16[4,2,4,32,2048]{4,3,2,1,0:T(8,128)(2,1)S(1)} %bitcast.33, bf16[1024,2048]{1,0:T(8,128)(2,1)S(1)} %fusion.4), kind=kOutput, calls=%fused_computation.1 | convolution fusion | flops 4294967296 | bytes 12582912 | tf_op jit(solution)/shard_map/dot_general | solution.py:476
  123.2 28.2 %sum_rows.1 = f32[32,1024]{1,0:T(8,128)} custom-call(f32[4,2,4,32,1024]{4,3,2,1,0:T(8,128)} %fusion.c_ref), custom_call_target="tpu_custom_call" | custom-call | tf_op jit(solution)/shard_map/sum_rows/pallas_call | solution.py:339
  151.3 0.0 all-gather.2.cloned.1.call-update
  152.0 4.7 %fusion.9 = f32[128,1024]{1,0:T(8,128)} fusion(bf16[1024,2048]{1,0:T(8,128)(2,1)} %copy-done, s32[]{:T(128)S(6)} %select_n.75), kind=kOutput, calls=%fused_computation.11 | convolution fusion | flops 536870912 | bytes 5242884 | tf_op jit(solution)/shard_map/dot_general | solution.py:475
  156.7 46.6 %sum_block.1 = f32[8,4,2,2,8,1024]{5,4,3,2,1,0:T(8,128)} custom-call(f32[4,2,2,8,1024]{4,3,2,1,0:T(8,128)} %bitcast.30), custom_call_target="tpu_custom_call" | custom-call | tf_op jit(solution)/shard_map/sum_block/pallas_call | solution.py:435
  203.4 0.2 select_reduce_fusion
  203.6 2.7 broadcast_multiply_fusion
  206.3 2.2 bitcast_add_fusion.a_ref
  208.5 61.6 %factor.1.f_ref = f32[1024,1024]{1,0:T(8,128)} custom-call(f32[1024,1024]{1,0:T(8,128)} %bitcast_add_fusion.a_ref), custom_call_target="tpu_custom_call" | custom-call | flops 42949672960 | bytes 8388608 | tf_op jit(solution)/shard_map/factor/pallas_call | solution.py:89
  270.1 0.0 all-gather.2.cloned.1.call-done
  270.1 2.9 gather_fusion
  273.0 0.7 select_add_fusion.g_ref
  273.7 7.6 %solve.1 = f32[32,1024]{1,0:T(8,128)} custom-call(f32[32,1024]{1,0:T(8,128)} %select_add_fusion.g_ref, f32[1024,1024]{1,0:T(8,128)} %factor.1.f_ref), custom_call_target="tpu_custom_call" | custom-call | tf_op jit(solution)/shard_map/solve/pallas_call | solution.py:113
  (6 shorter events, 0.1 us)
Async XLA Ops:
  6.5 263.6 %all-gather.2.cloned.1.call-start = ((), (), s32[]{:S(2)}) async-start(), calls=%async_computation | async-start | bytes 4325376 | tf_op jit(solution)/shard_map/all_gather | solution.py:478
  107.9 9.2 %copy-start.1 = (bf16[8,4,32,2048]{3,2,1,0:T(8,128)(2,1)S(1)}, bf16[8,4,32,2048]{3,2,1,0:T(8,128)(2,1)}, u32[]{:S(2)}) copy-start(bf16[8,4,32,2048]{3,2,1,0:T(8,128)(2,1)} %get-tuple-element.9) | copy-start | bytes 12582916
  115.1 2.0 copy-start
Sparse Core Ops, SparseCore 0:
  151.5 79.4 all-gather.1
